TPU v7x, 32 devices: a whole 2x2x4 slice. The times are simulated.
32 devices in a mesh: comp: 4 (over y, core), dom: 8 (over z, x).
Axes of the slice: x: 2, y: 2, z: 4, core: 2. Of those that a mesh axis runs over, the one named last changes fastest.
Arguments:
- source_field: bfloat16 [4, 8, 32, 16, 128], P('comp', 'dom'), may hold values from -108 to 108, as said below
- source_block: int32 [4, 8, 12], P('comp', 'dom'), may hold values from 0 to 31
- margin: int32 [4, 8, 12, 2], P('comp', 'dom'), may hold values from 0 to 31, as said below
- remap_weight: bfloat16 [4, 8, 12, 128, 128], P('comp', 'dom'), may hold values from 0 to 0.7, as said below
- helm_coef: float32 [256, 512], P('dom', 'comp'), may hold values from 0.05 to 1
Outputs:
- solution: float32 [16, 256, 512], P(None, 'dom', 'comp')
- residual: float32 [16, 256, 512], P(None, 'dom', 'comp')
Inputs may be any that keep to these rules, and one draw needn't show every extreme that they name: `source_field`: each value is a normal or uniform draw times scales that vary by field level, cell and device. `margin`: for each device and each owner, at most 4 of the device's entries name that owner and they name at most 2 distinct target rows; on every device some owner has exactly 4 entries. `remap_weight`: Nonnegative.
All inputs are finite; a program needn't handle non-finite values.
Results may differ from a plain program's by a relative error of at most 0.0003.
Values sent between devices are 32-bit elements; how exact they have to be, the bound alone decides.
No kernel may reach another device: no remote copies, remote signals or barrier semaphores. Data moves between devices by JAX's collectives and lax.ppermute only.
A program may use at most 64 MiB of HBM per device.

v0:
```python
import jax
import jax.numpy as jnp
from jax import lax
from jax.sharding import PartitionSpec as P

CAP = 4
ITERS = 2
HIGHEST = lax.Precision.HIGHEST


def with_halo(array, sides, width):
    for axis, dim in sides:
        devices, length = (lax.axis_size(axis), array.shape[dim])
        up = [(i, (i + 1) % devices) for i in range(devices - 1)]
        down = [(j, i) for i, j in up]
        last = lax.slice_in_dim(array, length - width, length, axis=dim)
        initial = lax.slice_in_dim(array, 0, width, axis=dim)
        before = lax.ppermute(last, axis, up)
        after = lax.ppermute(initial, axis, down)
        array = jnp.concatenate([before, array, after], axis=dim)
    return array


def row_dots(left, right):
    return jnp.sum(left * right, axis=(1, 2))


def operate(current, helm_coef):
    padded = with_halo(current, (("comp", 2), ("dom", 1)), 1)
    beside = padded[:, 2:, 1:-1] + padded[:, :-2, 1:-1] + padded[:, 1:-1, 2:] + padded[:, 1:-1, :-2]
    return (4.0 + helm_coef) * current - beside


def two_products(residual, applied):
    return lax.psum((row_dots(residual, residual), row_dots(residual, applied)), ("comp", "dom"))


def per_device(source_field, source_block, margin, remap_weight, helm_coef):
    sources = source_field[0, 0]
    block_ids = source_block[0, 0]
    peer_ids = margin[0, 0, :, 0]
    row_dest = margin[0, 0, :, 1]
    weights = remap_weight[0, 0]
    picked = jnp.take(sources, block_ids, axis=0)
    remapped = jnp.einsum("krs,kts->krt", picked, weights, preferred_element_type=jnp.float32)
    groups = lax.axis_size("comp")
    entries = peer_ids.shape[0]
    rows_here = helm_coef.shape[0]
    position = jnp.arange(entries, dtype=jnp.int32)
    earlier = position[None, :] < position[:, None]
    same_peer = peer_ids[:, None] == peer_ids[None, :]
    slot_ids = jnp.sum(earlier & same_peer, axis=1)
    slot_width = CAP
    slot_total = groups * slot_width
    placing = (
        (peer_ids * slot_width + slot_ids)[:, None]
        == jnp.arange(slot_total, dtype=jnp.int32)[None, :]
    ).astype(jnp.float32)
    outgoing = jnp.einsum("ks,krb->srb", placing, remapped, precision=HIGHEST)
    labels = jnp.max(placing * (row_dest + 1).astype(jnp.float32)[:, None], axis=0) - 1.0
    arrived, arrived_labels = (
        lax.all_to_all(outgoing, "comp", split_axis=0, concat_axis=0, tiled=True),
        lax.all_to_all(labels, "comp", split_axis=0, concat_axis=0, tiled=True),
    )
    landing = (
        arrived_labels.astype(jnp.int32)[:, None] == jnp.arange(rows_here, dtype=jnp.int32)[None, :]
    ).astype(jnp.float32)
    target = jnp.einsum("st,srb->rtb", landing, arrived, precision=HIGHEST)
    solution = jnp.zeros_like(target)
    residual = target
    applied = operate(residual, helm_coef)
    norm_now, product = two_products(residual, applied)
    step_len = norm_now / product
    direction = residual
    along = applied
    for step in range(ITERS):
        solution = solution + step_len[:, None, None] * direction
        residual = residual - step_len[:, None, None] * along
        if step + 1 < ITERS:
            applied = operate(residual, helm_coef)
            norm_next, product = two_products(residual, applied)
            ratio = norm_next / norm_now
            step_len = norm_next / (product - ratio * norm_next / step_len)
            direction = residual + ratio[:, None, None] * direction
            along = applied + ratio[:, None, None] * along
            norm_now = norm_next
    return (solution, residual)


def solution(mesh):
    placed = (
        P("comp", "dom", None, None, None),
        P("comp", "dom", None),
        P("comp", "dom", None, None),
        P("comp", "dom", None, None, None),
        P("dom", "comp"),
    )
    return jax.shard_map(
        per_device,
        mesh=mesh,
        in_specs=placed,
        out_specs=(P(None, "dom", "comp"), P(None, "dom", "comp")),
        check_vma=False,
    )
```

profile of v0, /device:TPU:0, one launch (start us, length us, event | category | flops | bytes accessed | tf_op | source)
XLA Modules:
  0.0 140.9 jit_solution(12832660203048157975)
XLA Ops:
  0.6 0.0 copy-start
  0.6 0.8 convert_bitcast_fusion
  1.4 0.0 copy-start.2
  1.4 0.2 convert_reduce_fusion
  1.6 0.5 copy-done.2
  2.1 0.1 select_reduce_fusion
  2.2 0.7 sub.21
  2.9 0.0 copy-start.3
  2.9 4.4 %all-to-all-start.1 = ((f32[4,4,1]{1,2,0:T(1,128)}), f32[4,4,1]{1,2,0:T(1,128)S(1)}, u32[]{:S(2)}, u32[]{:S(2)}) async-start(f32[4,4,1]{1,2,0:T(1,128)} %bitcast.8), calls=%async_computation.1 | async-start | bytes 4096 | tf_op jit(solution)/shard_map/all_to_all | solution.py:63
  7.2 0.0 copy-done.3
  7.3 1.5 %gather_fusion = bf16[12,16,128]{2,1,0:T(8,128)(2,1)S(1)} fusion(bf16[32,16,128]{2,1,0:T(8,128)(2,1)} %bitcast.25, s32[1024]{0:T(1024)S(1)} %pad_clamp_fusion), kind=kCustom, calls=%fused_computation | custom fusion | bytes 98352 | tf_op jit(solution)/shard_map/jit(_take)/gather | solution.py:44
  8.8 0.0 copy-done
  8.8 0.3 fusion
  9.1 0.3 fusion.11
  9.5 0.7 copy.11
  10.2 0.8 all-to-all-done.1
  11.0 3.3 %all-to-all-start = ((f32[16,16,128]{2,1,0:T(8,128)}), f32[16,16,128]{2,1,0:T(8,128)S(1)}, u32[]{:S(2)}, u32[]{:S(2)}) async-start(f32[16,16,128]{2,1,0:T(8,128)} %copy.11), calls=%async_computation | async-start | bytes 262144 | tf_op jit(solution)/shard_map/all_to_all | solution.py:62
  14.3 0.1 convert_element_type.29
  14.4 4.5 %all-to-all-done = f32[16,16,128]{2,1,0:T(8,128)S(1)} async-done(((f32[16,16,128]{2,1,0:T(8,128)}), f32[16,16,128]{2,1,0:T(8,128)S(1)}, u32[]{:S(2)}, u32[]{:S(2)}) %all-to-all-start) | async-done | bytes 131104 | tf_op jit(solution)/shard_map/all_to_all | solution.py:62
  18.9 0.4 convolution_bitcast_fusion
  19.2 0.1 fusion.27
  19.4 1.3 collective-permute-start.1
  20.7 0.0 copy-start.1
  20.7 3.0 %collective-permute-start = (f32[16,32,1]{2,1,0:T(8,128)S(1)}, f32[16,32,1]{2,1,0:T(8,128)S(1)}, u32[]{:S(2)}, u32[]{:S(2)}) collective-permute-start(f32[16,32,1]{2,1,0:T(8,128)S(1)} %get-tuple-element.22), channel_id=1, source_target_pairs={{0,8},{8,16},{16,24},{1,9},{9,17},{17,25},{2,10},{10,18},{18,26},{... | collective-permute-start | bytes 6152 | tf_op jit(solution)/shard_map/ppermute | solution.py:18
  23.8 0.0 collective-permute-done.1
  23.8 1.1 collective-permute-done
  24.9 0.2 pad_maximum_fusion.21
  25.1 1.3 collective-permute-start.2
  26.4 4.5 %collective-permute-start.3 = (f32[16,1,130]{2,1,0:T(1,128)S(1)}, f32[16,1,130]{2,1,0:T(1,128)S(1)}, u32[]{:S(2)}, u32[]{:S(2)}) collective-permute-start(f32[16,1,130]{2,1,0:T(1,128)S(1)} %get-tuple-element.16), channel_id=1, source_target_pairs={{0,1},{1,2},{2,3},{3,4},{4,5},{5,6},{6,7},{8,9},{9,10},{10,11},{11... | collective-permute-start | bytes 24968 | tf_op jit(solution)/shard_map/ppermute | solution.py:18
  30.9 0.0 copy-done.1
  30.9 0.0 collective-permute-done.2
  30.9 1.4 collective-permute-done.3
  32.3 0.8 multiply_reduce_fusion.2
  33.1 45.7 %all-reduce.1 = (f32[16]{0:T(128)S(1)}, f32[16]{0:T(128)S(1)}) all-reduce(f32[16]{0:T(128)S(1)} %get-tuple-element.5, f32[16]{0:T(128)S(1)} %get-tuple-element.4), channel_id=1, replica_groups=mesh['comp'=4,'dom'=8] {'comp','dom'}, use_global_device_ids=true, to_apply=%region_3.4 | all-reduce | flops 32 | bytes 256 | tf_op jit(solution)/shard_map/psum | solution.py:35
  78.8 0.1 multiply_subtract_fusion.1
  78.9 0.1 fusion.26
  79.1 1.3 collective-permute-start.5
  80.4 3.0 %collective-permute-start.4 = (f32[16,32,1]{2,1,0:T(8,128)S(1)}, f32[16,32,1]{2,1,0:T(8,128)S(1)}, u32[]{:S(2)}, u32[]{:S(2)}) collective-permute-start(f32[16,32,1]{2,1,0:T(8,128)S(1)} %get-tuple-element.20), channel_id=1, source_target_pairs={{0,8},{8,16},{16,24},{1,9},{9,17},{17,25},{2,10},{10,18},{18,26},{... | collective-permute-start | bytes 6152 | tf_op jit(solution)/shard_map/ppermute | solution.py:18
  83.4 0.0 collective-permute-done.5
  83.4 1.1 collective-permute-done.4
  84.5 0.2 pad_maximum_fusion.18
  84.7 1.3 collective-permute-start.6
  86.0 4.8 %collective-permute-start.7 = (f32[16,1,130]{2,1,0:T(1,128)S(1)}, f32[16,1,130]{2,1,0:T(1,128)S(1)}, u32[]{:S(2)}, u32[]{:S(2)}) collective-permute-start(f32[16,1,130]{2,1,0:T(1,128)S(1)} %get-tuple-element.14), channel_id=1, source_target_pairs={{0,1},{1,2},{2,3},{3,4},{4,5},{5,6},{6,7},{8,9},{9,10},{10,11},{11... | collective-permute-start | bytes 24968 | tf_op jit(solution)/shard_map/ppermute | solution.py:18
  90.8 0.0 collective-permute-done.6
  90.8 1.4 %collective-permute-done.7 = f32[16,1,130]{2,1,0:T(1,128)S(1)} collective-permute-done((f32[16,1,130]{2,1,0:T(1,128)S(1)}, f32[16,1,130]{2,1,0:T(1,128)S(1)}, u32[]{:S(2)}, u32[]{:S(2)}) %collective-permute-start.7) | collective-permute-done | bytes 8352 | tf_op jit(solution)/shard_map/ppermute | solution.py:18
  92.3 0.8 multiply_reduce_fusion
  93.0 46.6 %all-reduce = (f32[16]{0:T(128)S(1)}, f32[16]{0:T(128)S(1)}) all-reduce(f32[16]{0:T(128)S(1)} %get-tuple-element.3, f32[16]{0:T(128)S(1)} %get-tuple-element.2), channel_id=1, replica_groups=mesh['comp'=4,'dom'=8] {'comp','dom'}, use_global_device_ids=true, to_apply=%region_7.8 | all-reduce | flops 32 | bytes 256 | tf_op jit(solution)/shard_map/psum | solution.py:35
  139.6 1.2 multiply_subtract_fusion
  (9 shorter events, 0.1 us)
Async XLA Ops:
  0.6 8.1 %copy-start = (bf16[1,1,12,128,128]{4,3,2,1,0:T(8,128)(2,1)S(1)}, bf16[1,1,12,128,128]{4,3,2,1,0:T(8,128)(2,1)}, u32[]{:S(2)}) copy-start(bf16[1,1,12,128,128]{4,3,2,1,0:T(8,128)(2,1)} %param.8) | copy-start | bytes 1179652
  1.4 0.7 copy-start.2
  2.9 4.4 %copy-start.3 = (s32[1,1,12]{2,1,0:T(1,128)S(1)}, s32[1,1,12]{2,1,0:T(1,128)}, u32[]{:S(2)}) copy-start(s32[1,1,12]{2,1,0:T(1,128)} %param.6) | copy-start | bytes 148
  2.9 8.1 %all-to-all-start.1 = ((f32[4,4,1]{1,2,0:T(1,128)}), f32[4,4,1]{1,2,0:T(1,128)S(1)}, u32[]{:S(2)}, u32[]{:S(2)}) async-start(f32[4,4,1]{1,2,0:T(1,128)} %bitcast.8), calls=%async_computation.1 | async-start | bytes 4096 | tf_op jit(solution)/shard_map/all_to_all | solution.py:63
  11.0 7.9 %all-to-all-start = ((f32[16,16,128]{2,1,0:T(8,128)}), f32[16,16,128]{2,1,0:T(8,128)S(1)}, u32[]{:S(2)}, u32[]{:S(2)}) async-start(f32[16,16,128]{2,1,0:T(8,128)} %copy.11), calls=%async_computation | async-start | bytes 262144 | tf_op jit(solution)/shard_map/all_to_all | solution.py:62
  19.4 4.4 %collective-permute-start.1 = (f32[16,32,1]{2,1,0:T(8,128)S(1)}, f32[16,32,1]{2,1,0:T(8,128)S(1)}, u32[]{:S(2)}, u32[]{:S(2)}) collective-permute-start(f32[16,32,1]{2,1,0:T(8,128)S(1)} %get-tuple-element.21), channel_id=1, source_target_pairs={{8,0},{16,8},{24,16},{9,1},{17,9},{25,17},{10,2},{18,10},{26,18},{... | collective-permute-start | bytes 6152 | tf_op jit(solution)/shard_map/ppermute | solution.py:19
  20.7 10.2 %copy-start.1 = (f32[32,128]{1,0:T(8,128)S(1)}, f32[32,128]{1,0:T(8,128)}, u32[]{:S(2)}) copy-start(f32[32,128]{1,0:T(8,128)} %param.9) | copy-start | bytes 49156
  20.7 4.2 %collective-permute-start = (f32[16,32,1]{2,1,0:T(8,128)S(1)}, f32[16,32,1]{2,1,0:T(8,128)S(1)}, u32[]{:S(2)}, u32[]{:S(2)}) collective-permute-start(f32[16,32,1]{2,1,0:T(8,128)S(1)} %get-tuple-element.22), channel_id=1, source_target_pairs={{0,8},{8,16},{16,24},{1,9},{9,17},{17,25},{2,10},{10,18},{18,26},{... | collective-permute-start | bytes 6152 | tf_op jit(solution)/shard_map/ppermute | solution.py:18
  25.1 5.9 %collective-permute-start.2 = (f32[16,1,130]{2,1,0:T(1,128)S(1)}, f32[16,1,130]{2,1,0:T(1,128)S(1)}, u32[]{:S(2)}, u32[]{:S(2)}) collective-permute-start(f32[16,1,130]{2,1,0:T(1,128)S(1)} %get-tuple-element.15), channel_id=1, source_target_pairs={{1,0},{2,1},{3,2},{4,3},{5,4},{6,5},{7,6},{9,8},{10,9},{11,10},{12... | collective-permute-start | bytes 24968 | tf_op jit(solution)/shard_map/ppermute | solution.py:19
  26.4 6.0 %collective-permute-start.3 = (f32[16,1,130]{2,1,0:T(1,128)S(1)}, f32[16,1,130]{2,1,0:T(1,128)S(1)}, u32[]{:S(2)}, u32[]{:S(2)}) collective-permute-start(f32[16,1,130]{2,1,0:T(1,128)S(1)} %get-tuple-element.16), channel_id=1, source_target_pairs={{0,1},{1,2},{2,3},{3,4},{4,5},{5,6},{6,7},{8,9},{9,10},{10,11},{11... | collective-permute-start | bytes 24968 | tf_op jit(solution)/shard_map/ppermute | solution.py:18
  79.1 4.4 %collective-permute-start.5 = (f32[16,32,1]{2,1,0:T(8,128)S(1)}, f32[16,32,1]{2,1,0:T(8,128)S(1)}, u32[]{:S(2)}, u32[]{:S(2)}) collective-permute-start(f32[16,32,1]{2,1,0:T(8,128)S(1)} %get-tuple-element.19), channel_id=1, source_target_pairs={{8,0},{16,8},{24,16},{9,1},{17,9},{25,17},{10,2},{18,10},{26,18},{... | collective-permute-start | bytes 6152 | tf_op jit(solution)/shard_map/ppermute | solution.py:19
  80.4 4.2 %collective-permute-start.4 = (f32[16,32,1]{2,1,0:T(8,128)S(1)}, f32[16,32,1]{2,1,0:T(8,128)S(1)}, u32[]{:S(2)}, u32[]{:S(2)}) collective-permute-start(f32[16,32,1]{2,1,0:T(8,128)S(1)} %get-tuple-element.20), channel_id=1, source_target_pairs={{0,8},{8,16},{16,24},{1,9},{9,17},{17,25},{2,10},{10,18},{18,26},{... | collective-permute-start | bytes 6152 | tf_op jit(solution)/shard_map/ppermute | solution.py:18
  84.7 6.1 %collective-permute-start.6 = (f32[16,1,130]{2,1,0:T(1,128)S(1)}, f32[16,1,130]{2,1,0:T(1,128)S(1)}, u32[]{:S(2)}, u32[]{:S(2)}) collective-permute-start(f32[16,1,130]{2,1,0:T(1,128)S(1)} %get-tuple-element.13), channel_id=1, source_target_pairs={{1,0},{2,1},{3,2},{4,3},{5,4},{6,5},{7,6},{9,8},{10,9},{11,10},{12... | collective-permute-start | bytes 24968 | tf_op jit(solution)/shard_map/ppermute | solution.py:19
  86.0 6.2 %collective-permute-start.7 = (f32[16,1,130]{2,1,0:T(1,128)S(1)}, f32[16,1,130]{2,1,0:T(1,128)S(1)}, u32[]{:S(2)}, u32[]{:S(2)}) collective-permute-start(f32[16,1,130]{2,1,0:T(1,128)S(1)} %get-tuple-element.14), channel_id=1, source_target_pairs={{0,1},{1,2},{2,3},{3,4},{4,5},{5,6},{6,7},{8,9},{9,10},{10,11},{11... | collective-permute-start | bytes 24968 | tf_op jit(solution)/shard_map/ppermute | solution.py:18
where the time goes:
time: 141 us
  blocking collectives  92.3 us (65%)
  starting transfers between devices  28.3 us (20%)
  waiting for transfers between devices  10.3 us (7%)
  other arithmetic  4.26 us (3%)
  local copies, waits for them, and re-layouts  3.7 us (3%)
    psum x2, blocking collectives, two_products(): lax.psum((row_dots(residual, residual), row_dots(residual, applied)), ('c...  92.3 us
    ppermute x4, starting transfers between devices, with_halo(): before = lax.ppermute(last, axis, up)  15.4 us
    ppermute x4, starting transfers between devices, with_halo(): after = lax.ppermute(initial, axis, down)  5.17 us
    ppermute x4, waiting for transfers between devices, with_halo(): before = lax.ppermute(last, axis, up)  5.04 us
    all_to_all x1, waiting for transfers between devices, per_device(): lax.all_to_all(outgoing, 'comp', split_axis=0, concat_axis=0, tiled=True)  4.46 us
    all_to_all x1, starting transfers between devices, per_device(): lax.all_to_all(labels, 'comp', split_axis=0, concat_axis=0, tiled=True)  4.4 us
    all_to_all x1, starting transfers between devices, per_device(): lax.all_to_all(outgoing, 'comp', split_axis=0, concat_axis=0, tiled=True)  3.33 us
  transfers between devices with their start and end apart: 10, of which 6 were waited for; matrix products, arithmetic and copies ran while one was open for 2% of the time, Pallas kernels for 0%

commit v1 on v0

--- a/solution.py
+++ b/solution.py
@@ -32,7 +32,9 @@
 
 
 def two_products(residual, applied):
-    return lax.psum((row_dots(residual, residual), row_dots(residual, applied)), ("comp", "dom"))
+    return lax.psum(
+        lax.psum((row_dots(residual, residual), row_dots(residual, applied)), "dom"), "comp"
+    )
 
 
 def per_device(source_field, source_block, margin, remap_weight, helm_coef):

time: 141 us -> 110 us (0.78)
  blocking collectives: 92.3 us -> 60.9 us
    psum x2 -> x4, blocking collectives: 92.3 us -> 60.9 us  [the longest x2 42.3 us: two_products(): lax.psum((row_dots(residual, residual), row_dots(residual, applied)), 'dom')]
  transfers between devices with their start and end apart: 10 -> 10, of which waited for: 6 -> 6; matrix products, arithmetic and copies ran while one was open for 2% -> 3% of each run, Pallas kernels for 0% -> 0%
where the time goes in v1:
time: 110 us; the launch traced here: 109 us
  blocking collectives  60.9 us (55%)
  starting transfers between devices  28.1 us (26%)
  waiting for transfers between devices  10.3 us (9%)
  other arithmetic  4.27 us (4%)
  local copies, waits for them, and re-layouts  3.7 us (3%)
    psum x2, blocking collectives, two_products(): lax.psum((row_dots(residual, residual), row_dots(residual, applied)), 'dom')  42.3 us
    psum x2, blocking collectives, two_products(): lax.psum(lax.psum((row_dots(residual, residual), row_dots(residual, appli...  18.7 us
    ppermute x4, starting transfers between devices, with_halo(): before = lax.ppermute(last, axis, up)  15.2 us
    ppermute x4, starting transfers between devices, with_halo(): after = lax.ppermute(initial, axis, down)  5.17 us
    ppermute x4, waiting for transfers between devices, with_halo(): before = lax.ppermute(last, axis, up)  5.04 us
    all_to_all x1, waiting for transfers between devices, per_device(): lax.all_to_all(outgoing, 'comp', split_axis=0, concat_axis=0, tiled=True)  4.46 us
    all_to_all x1, starting transfers between devices, per_device(): lax.all_to_all(labels, 'comp', split_axis=0, concat_axis=0, tiled=True)  4.4 us
    all_to_all x1, starting transfers between devices, per_device(): lax.all_to_all(outgoing, 'comp', split_axis=0, concat_axis=0, tiled=True)  3.33 us
  transfers between devices with their start and end apart: 10, of which 6 were waited for; matrix products, arithmetic and copies ran while one was open for 3% of the time, Pallas kernels for 0%

profile of v1, /device:TPU:0, one launch (start us, length us, event | category | flops | bytes accessed | tf_op | source)
XLA Modules:
  0.0 109.2 jit_solution(13379285308597822890)
XLA Ops:
  0.6 0.0 copy-start
  0.6 0.8 convert_bitcast_fusion
  1.4 0.2 convert_reduce_fusion
  1.6 0.5 copy-done.2
  2.1 0.1 select_reduce_fusion
  2.2 0.7 sub.21
  2.9 4.4 %all-to-all-start.1 = ((f32[4,4,1]{1,2,0:T(1,128)}), f32[4,4,1]{1,2,0:T(1,128)S(1)}, u32[]{:S(2)}, u32[]{:S(2)}) async-start(f32[4,4,1]{1,2,0:T(1,128)} %bitcast.8), calls=%async_computation.1 | async-start | bytes 4096 | tf_op jit(solution)/shard_map/all_to_all | solution.py:65
  7.2 0.0 copy-done.3
  7.3 1.5 %gather_fusion = bf16[12,16,128]{2,1,0:T(8,128)(2,1)S(1)} fusion(bf16[32,16,128]{2,1,0:T(8,128)(2,1)} %bitcast.25, s32[1024]{0:T(1024)S(1)} %pad_clamp_fusion), kind=kCustom, calls=%fused_computation | custom fusion | bytes 98352 | tf_op jit(solution)/shard_map/jit(_take)/gather | solution.py:46
  8.8 0.0 copy-done
  8.8 0.3 fusion
  9.1 0.3 fusion.11
  9.5 0.7 copy.11
  10.2 0.8 all-to-all-done.1
  11.0 3.3 %all-to-all-start = ((f32[16,16,128]{2,1,0:T(8,128)}), f32[16,16,128]{2,1,0:T(8,128)S(1)}, u32[]{:S(2)}, u32[]{:S(2)}) async-start(f32[16,16,128]{2,1,0:T(8,128)} %copy.11), calls=%async_computation | async-start | bytes 262144 | tf_op jit(solution)/shard_map/all_to_all | solution.py:64
  14.3 0.1 convert_element_type.29
  14.4 4.5 %all-to-all-done = f32[16,16,128]{2,1,0:T(8,128)S(1)} async-done(((f32[16,16,128]{2,1,0:T(8,128)}), f32[16,16,128]{2,1,0:T(8,128)S(1)}, u32[]{:S(2)}, u32[]{:S(2)}) %all-to-all-start) | async-done | bytes 131104 | tf_op jit(solution)/shard_map/all_to_all | solution.py:64
  18.9 0.4 convolution_bitcast_fusion
  19.2 0.1 fusion.27
  19.4 1.3 %collective-permute-start.1 = (f32[16,32,1]{2,1,0:T(8,128)S(1)}, f32[16,32,1]{2,1,0:T(8,128)S(1)}, u32[]{:S(2)}, u32[]{:S(2)}) collective-permute-start(f32[16,32,1]{2,1,0:T(8,128)S(1)} %get-tuple-element.25), channel_id=1, source_target_pairs={{8,0},{16,8},{24,16},{9,1},{17,9},{25,17},{10,2},{18,10},{26,18},{... | collective-permute-start | bytes 6152 | tf_op jit(solution)/shard_map/ppermute | solution.py:19
  20.7 0.0 copy-start.1
  20.7 3.0 %collective-permute-start = (f32[16,32,1]{2,1,0:T(8,128)S(1)}, f32[16,32,1]{2,1,0:T(8,128)S(1)}, u32[]{:S(2)}, u32[]{:S(2)}) collective-permute-start(f32[16,32,1]{2,1,0:T(8,128)S(1)} %get-tuple-element.26), channel_id=1, source_target_pairs={{0,8},{8,16},{16,24},{1,9},{9,17},{17,25},{2,10},{10,18},{18,26},{... | collective-permute-start | bytes 6152 | tf_op jit(solution)/shard_map/ppermute | solution.py:18
  23.8 0.0 collective-permute-done.1
  23.8 1.1 %collective-permute-done = f32[16,32,1]{2,1,0:T(8,128)S(1)} collective-permute-done((f32[16,32,1]{2,1,0:T(8,128)S(1)}, f32[16,32,1]{2,1,0:T(8,128)S(1)}, u32[]{:S(2)}, u32[]{:S(2)}) %collective-permute-start) | collective-permute-done | bytes 2080 | tf_op jit(solution)/shard_map/ppermute | solution.py:18
  24.9 0.2 pad_maximum_fusion.21
  25.1 1.3 %collective-permute-start.2 = (f32[16,1,130]{2,1,0:T(1,128)S(1)}, f32[16,1,130]{2,1,0:T(1,128)S(1)}, u32[]{:S(2)}, u32[]{:S(2)}) collective-permute-start(f32[16,1,130]{2,1,0:T(1,128)S(1)} %get-tuple-element.19), channel_id=1, source_target_pairs={{1,0},{2,1},{3,2},{4,3},{5,4},{6,5},{7,6},{9,8},{10,9},{11,10},{12... | collective-permute-start | bytes 24968 | tf_op jit(solution)/shard_map/ppermute | solution.py:19
  26.4 4.5 %collective-permute-start.3 = (f32[16,1,130]{2,1,0:T(1,128)S(1)}, f32[16,1,130]{2,1,0:T(1,128)S(1)}, u32[]{:S(2)}, u32[]{:S(2)}) collective-permute-start(f32[16,1,130]{2,1,0:T(1,128)S(1)} %get-tuple-element.20), channel_id=1, source_target_pairs={{0,1},{1,2},{2,3},{3,4},{4,5},{5,6},{6,7},{8,9},{9,10},{10,11},{11... | collective-permute-start | bytes 24968 | tf_op jit(solution)/shard_map/ppermute | solution.py:18
  30.9 0.0 copy-done.1
  30.9 0.0 collective-permute-done.2
  30.9 1.4 %collective-permute-done.3 = f32[16,1,130]{2,1,0:T(1,128)S(1)} collective-permute-done((f32[16,1,130]{2,1,0:T(1,128)S(1)}, f32[16,1,130]{2,1,0:T(1,128)S(1)}, u32[]{:S(2)}, u32[]{:S(2)}) %collective-permute-start.3) | collective-permute-done | bytes 8352 | tf_op jit(solution)/shard_map/ppermute | solution.py:18
  32.3 0.8 multiply_reduce_fusion.2
  33.1 22.8 %all-reduce.1 = (f32[16]{0:T(128)S(1)}, f32[16]{0:T(128)S(1)}) all-reduce(f32[16]{0:T(128)S(1)} %get-tuple-element.5, f32[16]{0:T(128)S(1)} %get-tuple-element.4), channel_id=1, replica_groups=mesh['comp'=4,'dom'=8] {'dom'}, use_global_device_ids=true, to_apply=%region_3.4 | all-reduce | flops 32 | bytes 256 | tf_op jit(solution)/shard_map/psum | solution.py:36
  55.9 8.8 %all-reduce.3 = (f32[16]{0:T(128)S(1)}, f32[16]{0:T(128)S(1)}) all-reduce(f32[16]{0:T(128)S(1)} %get-tuple-element.8, f32[16]{0:T(128)S(1)} %get-tuple-element.9), channel_id=1, replica_groups=mesh['comp'=4,'dom'=8] {'comp'}, use_global_device_ids=true, to_apply=%region_4.5 | all-reduce | flops 32 | bytes 256 | tf_op jit(solution)/shard_map/psum | solution.py:35
  64.7 0.1 multiply_subtract_fusion.1
  64.8 0.1 fusion.26
  64.9 1.3 %collective-permute-start.5 = (f32[16,32,1]{2,1,0:T(8,128)S(1)}, f32[16,32,1]{2,1,0:T(8,128)S(1)}, u32[]{:S(2)}, u32[]{:S(2)}) collective-permute-start(f32[16,32,1]{2,1,0:T(8,128)S(1)} %get-tuple-element.23), channel_id=1, source_target_pairs={{8,0},{16,8},{24,16},{9,1},{17,9},{25,17},{10,2},{18,10},{26,18},{... | collective-permute-start | bytes 6152 | tf_op jit(solution)/shard_map/ppermute | solution.py:19
  66.2 3.0 %collective-permute-start.4 = (f32[16,32,1]{2,1,0:T(8,128)S(1)}, f32[16,32,1]{2,1,0:T(8,128)S(1)}, u32[]{:S(2)}, u32[]{:S(2)}) collective-permute-start(f32[16,32,1]{2,1,0:T(8,128)S(1)} %get-tuple-element.24), channel_id=1, source_target_pairs={{0,8},{8,16},{16,24},{1,9},{9,17},{17,25},{2,10},{10,18},{18,26},{... | collective-permute-start | bytes 6152 | tf_op jit(solution)/shard_map/ppermute | solution.py:18
  69.3 0.0 collective-permute-done.5
  69.3 1.1 %collective-permute-done.4 = f32[16,32,1]{2,1,0:T(8,128)S(1)} collective-permute-done((f32[16,32,1]{2,1,0:T(8,128)S(1)}, f32[16,32,1]{2,1,0:T(8,128)S(1)}, u32[]{:S(2)}, u32[]{:S(2)}) %collective-permute-start.4) | collective-permute-done | bytes 2080 | tf_op jit(solution)/shard_map/ppermute | solution.py:18
  70.4 0.2 pad_maximum_fusion.18
  70.6 1.3 %collective-permute-start.6 = (f32[16,1,130]{2,1,0:T(1,128)S(1)}, f32[16,1,130]{2,1,0:T(1,128)S(1)}, u32[]{:S(2)}, u32[]{:S(2)}) collective-permute-start(f32[16,1,130]{2,1,0:T(1,128)S(1)} %get-tuple-element.17), channel_id=1, source_target_pairs={{1,0},{2,1},{3,2},{4,3},{5,4},{6,5},{7,6},{9,8},{10,9},{11,10},{12... | collective-permute-start | bytes 24968 | tf_op jit(solution)/shard_map/ppermute | solution.py:19
  71.9 4.5 %collective-permute-start.7 = (f32[16,1,130]{2,1,0:T(1,128)S(1)}, f32[16,1,130]{2,1,0:T(1,128)S(1)}, u32[]{:S(2)}, u32[]{:S(2)}) collective-permute-start(f32[16,1,130]{2,1,0:T(1,128)S(1)} %get-tuple-element.18), channel_id=1, source_target_pairs={{0,1},{1,2},{2,3},{3,4},{4,5},{5,6},{6,7},{8,9},{9,10},{10,11},{11... | collective-permute-start | bytes 24968 | tf_op jit(solution)/shard_map/ppermute | solution.py:18
  76.5 0.0 collective-permute-done.6
  76.5 1.4 %collective-permute-done.7 = f32[16,1,130]{2,1,0:T(1,128)S(1)} collective-permute-done((f32[16,1,130]{2,1,0:T(1,128)S(1)}, f32[16,1,130]{2,1,0:T(1,128)S(1)}, u32[]{:S(2)}, u32[]{:S(2)}) %collective-permute-start.7) | collective-permute-done | bytes 8352 | tf_op jit(solution)/shard_map/ppermute | solution.py:18
  77.9 0.8 multiply_reduce_fusion
  78.6 19.4 %all-reduce = (f32[16]{0:T(128)S(1)}, f32[16]{0:T(128)S(1)}) all-reduce(f32[16]{0:T(128)S(1)} %get-tuple-element.3, f32[16]{0:T(128)S(1)} %get-tuple-element.2), channel_id=1, replica_groups=mesh['comp'=4,'dom'=8] {'dom'}, use_global_device_ids=true, to_apply=%region_9.10 | all-reduce | flops 32 | bytes 256 | tf_op jit(solution)/shard_map/psum | solution.py:36
  98.0 9.9 %all-reduce.2 = (f32[16]{0:T(128)S(1)}, f32[16]{0:T(128)S(1)}) all-reduce(f32[16]{0:T(128)S(1)} %get-tuple-element.6, f32[16]{0:T(128)S(1)} %get-tuple-element.7), channel_id=1, replica_groups=mesh['comp'=4,'dom'=8] {'comp'}, use_global_device_ids=true, to_apply=%region_10.11 | all-reduce | flops 32 | bytes 256 | tf_op jit(solution)/shard_map/psum | solution.py:35
  108.0 1.2 %multiply_subtract_fusion = (f32[16,32,128]{2,1,0:T(8,128)}, f32[16,32,128]{2,1,0:T(8,128)}) fusion(f32[16,32,128]{2,1,0:T(8,128)S(1)} %multiply_subtract_fusion.1, f32[16,32,128]{2,1,0:T(8,128)S(1)} %get-tuple-element.16, f32[16]{0:T(128)S(1)} %get-tuple-element.15, f32[16]{0:T(128)S(1)} %get-tuple-element.14, f32[16,32,1]{2,1,0:T(8,128)S(1)} %collective-permute-done.4, ...), kind=kLoop, calls=%fused_computation.28 | loop fusion | flops 1441792 | bytes 1348032 | tf_op jit(solution)/shard_map/sub | solution.py:80
  (11 shorter events, 0.1 us)
Async XLA Ops:
  0.6 8.1 %copy-start = (bf16[1,1,12,128,128]{4,3,2,1,0:T(8,128)(2,1)S(1)}, bf16[1,1,12,128,128]{4,3,2,1,0:T(8,128)(2,1)}, u32[]{:S(2)}) copy-start(bf16[1,1,12,128,128]{4,3,2,1,0:T(8,128)(2,1)} %param.8) | copy-start | bytes 1179652
  1.4 0.7 copy-start.2
  2.9 4.4 %copy-start.3 = (s32[1,1,12]{2,1,0:T(1,128)S(1)}, s32[1,1,12]{2,1,0:T(1,128)}, u32[]{:S(2)}) copy-start(s32[1,1,12]{2,1,0:T(1,128)} %param.6) | copy-start | bytes 148
  2.9 8.1 %all-to-all-start.1 = ((f32[4,4,1]{1,2,0:T(1,128)}), f32[4,4,1]{1,2,0:T(1,128)S(1)}, u32[]{:S(2)}, u32[]{:S(2)}) async-start(f32[4,4,1]{1,2,0:T(1,128)} %bitcast.8), calls=%async_computation.1 | async-start | bytes 4096 | tf_op jit(solution)/shard_map/all_to_all | solution.py:65
  11.0 7.9 %all-to-all-start = ((f32[16,16,128]{2,1,0:T(8,128)}), f32[16,16,128]{2,1,0:T(8,128)S(1)}, u32[]{:S(2)}, u32[]{:S(2)}) async-start(f32[16,16,128]{2,1,0:T(8,128)} %copy.11), calls=%async_computation | async-start | bytes 262144 | tf_op jit(solution)/shard_map/all_to_all | solution.py:64
  19.4 4.4 %collective-permute-start.1 = (f32[16,32,1]{2,1,0:T(8,128)S(1)}, f32[16,32,1]{2,1,0:T(8,128)S(1)}, u32[]{:S(2)}, u32[]{:S(2)}) collective-permute-start(f32[16,32,1]{2,1,0:T(8,128)S(1)} %get-tuple-element.25), channel_id=1, source_target_pairs={{8,0},{16,8},{24,16},{9,1},{17,9},{25,17},{10,2},{18,10},{26,18},{... | collective-permute-start | bytes 6152 | tf_op jit(solution)/shard_map/ppermute | solution.py:19
  20.7 10.2 %copy-start.1 = (f32[32,128]{1,0:T(8,128)S(1)}, f32[32,128]{1,0:T(8,128)}, u32[]{:S(2)}) copy-start(f32[32,128]{1,0:T(8,128)} %param.9) | copy-start | bytes 49156
  20.7 4.2 %collective-permute-start = (f32[16,32,1]{2,1,0:T(8,128)S(1)}, f32[16,32,1]{2,1,0:T(8,128)S(1)}, u32[]{:S(2)}, u32[]{:S(2)}) collective-permute-start(f32[16,32,1]{2,1,0:T(8,128)S(1)} %get-tuple-element.26), channel_id=1, source_target_pairs={{0,8},{8,16},{16,24},{1,9},{9,17},{17,25},{2,10},{10,18},{18,26},{... | collective-permute-start | bytes 6152 | tf_op jit(solution)/shard_map/ppermute | solution.py:18
  25.1 5.9 %collective-permute-start.2 = (f32[16,1,130]{2,1,0:T(1,128)S(1)}, f32[16,1,130]{2,1,0:T(1,128)S(1)}, u32[]{:S(2)}, u32[]{:S(2)}) collective-permute-start(f32[16,1,130]{2,1,0:T(1,128)S(1)} %get-tuple-element.19), channel_id=1, source_target_pairs={{1,0},{2,1},{3,2},{4,3},{5,4},{6,5},{7,6},{9,8},{10,9},{11,10},{12... | collective-permute-start | bytes 24968 | tf_op jit(solution)/shard_map/ppermute | solution.py:19
  26.4 6.0 %collective-permute-start.3 = (f32[16,1,130]{2,1,0:T(1,128)S(1)}, f32[16,1,130]{2,1,0:T(1,128)S(1)}, u32[]{:S(2)}, u32[]{:S(2)}) collective-permute-start(f32[16,1,130]{2,1,0:T(1,128)S(1)} %get-tuple-element.20), channel_id=1, source_target_pairs={{0,1},{1,2},{2,3},{3,4},{4,5},{5,6},{6,7},{8,9},{9,10},{10,11},{11... | collective-permute-start | bytes 24968 | tf_op jit(solution)/shard_map/ppermute | solution.py:18
  64.9 4.4 %collective-permute-start.5 = (f32[16,32,1]{2,1,0:T(8,128)S(1)}, f32[16,32,1]{2,1,0:T(8,128)S(1)}, u32[]{:S(2)}, u32[]{:S(2)}) collective-permute-start(f32[16,32,1]{2,1,0:T(8,128)S(1)} %get-tuple-element.23), channel_id=1, source_target_pairs={{8,0},{16,8},{24,16},{9,1},{17,9},{25,17},{10,2},{18,10},{26,18},{... | collective-permute-start | bytes 6152 | tf_op jit(solution)/shard_map/ppermute | solution.py:19
  66.2 4.2 %collective-permute-start.4 = (f32[16,32,1]{2,1,0:T(8,128)S(1)}, f32[16,32,1]{2,1,0:T(8,128)S(1)}, u32[]{:S(2)}, u32[]{:S(2)}) collective-permute-start(f32[16,32,1]{2,1,0:T(8,128)S(1)} %get-tuple-element.24), channel_id=1, source_target_pairs={{0,8},{8,16},{16,24},{1,9},{9,17},{17,25},{2,10},{10,18},{18,26},{... | collective-permute-start | bytes 6152 | tf_op jit(solution)/shard_map/ppermute | solution.py:18
  70.6 5.9 %collective-permute-start.6 = (f32[16,1,130]{2,1,0:T(1,128)S(1)}, f32[16,1,130]{2,1,0:T(1,128)S(1)}, u32[]{:S(2)}, u32[]{:S(2)}) collective-permute-start(f32[16,1,130]{2,1,0:T(1,128)S(1)} %get-tuple-element.17), channel_id=1, source_target_pairs={{1,0},{2,1},{3,2},{4,3},{5,4},{6,5},{7,6},{9,8},{10,9},{11,10},{12... | collective-permute-start | bytes 24968 | tf_op jit(solution)/shard_map/ppermute | solution.py:19
  71.9 6.0 %collective-permute-start.7 = (f32[16,1,130]{2,1,0:T(1,128)S(1)}, f32[16,1,130]{2,1,0:T(1,128)S(1)}, u32[]{:S(2)}, u32[]{:S(2)}) collective-permute-start(f32[16,1,130]{2,1,0:T(1,128)S(1)} %get-tuple-element.18), channel_id=1, source_target_pairs={{0,1},{1,2},{2,3},{3,4},{4,5},{5,6},{6,7},{8,9},{9,10},{10,11},{11... | collective-permute-start | bytes 24968 | tf_op jit(solution)/shard_map/ppermute | solution.py:18
